TPU v7x, 256 devices: a whole 4x4x8 slice. The times are simulated.
256 devices in a mesh: ctx: 32 (over z, x_hi, core), head: 8 (over y, x_lo).
Axes of the slice: x: 4 (x_hi: 2, x_lo: 2; x = x_hi * 2 + x_lo), y: 4, z: 8, core: 2. Of those that a mesh axis runs over, the one named last changes fastest.
Arguments:
- queries: bfloat16 [8192, 8192], P('ctx', 'head'), may hold values from -10 to 10
- key_rows: bfloat16 [8192, 1024], P('ctx', 'head'), may hold values from -4.5 to 4.5
- values: bfloat16 [8192, 1024], P('ctx', 'head'), may hold values from -24 to 24
- lengths: int32 [17], replicated, may hold values from 1 to 4352, as said below
- block_plan: int32 [1024], P('ctx'), may hold values from 0 to 1023, as said below
- inverse: int32 [1024], replicated, may hold values from 0 to 1023, as said below
- mask_lo: int32 [1024], replicated, may hold values from 0 to 1023, as said below
- out_weight: bfloat16 [8192, 4096], P('head'), may hold values from -0.375 to 0.375
Outputs:
- mixed_out: bfloat16 [8192, 4096], P('ctx', 'head')
Inputs may be any that keep to these rules, and one draw needn't show every extreme that they name: One document has exactly 4352 tokens, every other is shorter; the lengths sum to 8192. A permutation of the 1024 blocks; slot block_plan[b] lies on index block_plan[b] // 32 of ctx; every index receives exactly 32 blocks, and at most 2 blocks of one index go to any one index, which is reached in every draw. inverse[block_plan[b]] == b. mask_lo[b] lies between the block holding the first token of the document of block b's first token and b, both included.
All inputs are finite; a program needn't handle non-finite values.
Results may differ from a plain program's by a relative error of at most 0.02.
Values may be sent and summed in bfloat16 or wider, within the bound.
A program may use at most 64 MiB of HBM per device.

v0:
```python
import jax
import jax.numpy as jnp
from jax import lax
from jax.sharding import PartitionSpec as P

HD = 128
BLK = 8
NEG_FILL = -1e30


def document_of(positions, doc_ends):
    return jnp.sum((positions[:, None] >= doc_ends[None, :]).astype(jnp.int32), axis=1)


def rank_within(owners, order_keys):
    same_owner = owners[:, None] == owners[None, :]
    comes_first = order_keys[None, :] < order_keys[:, None]
    return jnp.sum((same_owner & comes_first).astype(jnp.int32), axis=1)


def slot_sources(owners, order_ranks, device_count, capacity):
    device_ids = jnp.arange(device_count, dtype=jnp.int32)
    slot_ids = jnp.arange(capacity, dtype=jnp.int32)
    entry_ids = jnp.arange(owners.shape[0], dtype=jnp.int32)
    matches = (owners[None, None, :] == device_ids[:, None, None]) & (
        order_ranks[None, None, :] == slot_ids[None, :, None]
    )
    sources = jnp.sum(jnp.where(matches, entry_ids[None, None, :], 0), axis=2)
    return (sources.reshape(-1), jnp.any(matches, axis=2).reshape(-1))


def pack_blocks(block_data, sources, occupied, device_count, capacity):
    picked = jnp.take(block_data, sources, axis=0)
    picked = jnp.where(occupied[:, None, None], picked, jnp.zeros((), block_data.dtype))
    return picked.reshape((device_count, capacity) + block_data.shape[1:])


def unpack_blocks(received, owners, order_ranks, capacity):
    merged = received.reshape((-1,) + received.shape[2:])
    picked = jnp.take(merged, owners * capacity + order_ranks, axis=0)
    return picked.reshape((-1, picked.shape[-1]))


def project(attended, out_weight):
    partial_value = jnp.dot(attended, out_weight, preferred_element_type=jnp.float32).astype(
        jnp.bfloat16
    )
    summed = lax.psum_scatter(partial_value, "head", scatter_dimension=1, tiled=True).astype(
        jnp.float32
    )
    return summed.astype(jnp.bfloat16)


def attend_all(held_queries, held_pairs, root, doc_ends, mask_lo, key_position):
    row_count, query_width = held_queries.shape
    kv_width = held_pairs.shape[1] // 2
    kv_heads = kv_width // HD
    group_size = query_width // (kv_heads * HD)
    score_scale = HD ** (-0.5)
    offsets = jnp.arange(BLK, dtype=jnp.int32)
    query_pos = (root[:, None] * BLK + offsets[None, :]).reshape(row_count)
    query_doc = document_of(query_pos, doc_ends)
    table_ids = jnp.arange(mask_lo.shape[0], dtype=jnp.int32)
    block_lo = jnp.sum(jnp.where(root[:, None] == table_ids[None, :], mask_lo[None, :], 0), axis=1)
    query_lo = jnp.repeat(block_lo, BLK)
    query_heads = held_queries.reshape(row_count, kv_heads, group_size, HD)

    def one_step(state_now, kv_piece, first_key):
        key_width = kv_piece.shape[0]
        key_ids = first_key + jnp.arange(key_width, dtype=jnp.int32)
        key_pos = key_position(key_ids)
        key_doc = document_of(key_pos, doc_ends)
        allowed = (
            (query_doc[:, None] == key_doc[None, :])
            & (key_pos[None, :] <= query_pos[:, None])
            & ((key_pos // BLK)[None, :] >= query_lo[:, None])
        )
        run_max, run_sum, run_acc = state_now
        key_heads = kv_piece[:, :kv_width].reshape(key_width, kv_heads, HD)
        value_heads = kv_piece[:, kv_width:].reshape(key_width, kv_heads, HD)
        scores = (
            jnp.einsum("tkgd,skd->tkgs", query_heads, key_heads, preferred_element_type=jnp.float32)
            * score_scale
        )
        mask_full = allowed[:, None, None, :]
        scores = jnp.where(mask_full, scores, NEG_FILL)
        new_max = jnp.maximum(run_max, jnp.max(scores, axis=-1))
        weights = jnp.where(mask_full, jnp.exp(scores - new_max[..., None]), 0.0)
        fading = jnp.exp(run_max - new_max)
        new_sum = run_sum * fading + jnp.sum(weights, axis=-1)
        update = jnp.einsum(
            "tkgs,skd->tkgd",
            weights.astype(jnp.bfloat16),
            value_heads,
            preferred_element_type=jnp.float32,
        )
        return (new_max, new_sum, run_acc * fading[..., None] + update)

    stat_shape = (row_count, kv_heads, group_size)
    initial = (
        jnp.full(stat_shape, NEG_FILL, jnp.float32),
        jnp.zeros(stat_shape, jnp.float32),
        jnp.zeros(stat_shape + (HD,), jnp.float32),
    )
    kv_piece = lax.all_gather(held_pairs, "ctx", axis=0, tiled=True)
    piece_rows = kv_piece.shape[0]
    key_width = 256

    def loop_body(step_index, state_in):
        offset_rows = step_index * key_width
        sub_piece = lax.dynamic_slice_in_dim(kv_piece, offset_rows, key_width, 0)
        return one_step(state_in, sub_piece, offset_rows)

    run_max, run_sum, run_acc = lax.fori_loop(0, piece_rows // key_width, loop_body, initial)
    return (run_acc / run_sum[..., None]).astype(jnp.bfloat16).reshape(row_count, query_width)


def on_device(queries, key_rows, values, lengths, block_plan, inverse, mask_lo, out_weight):
    row_count, query_width = queries.shape
    block_count = row_count // BLK
    device_count = lax.axis_size("ctx")
    capacity = max(2, block_count // device_count + 1)
    here_index = lax.axis_index("ctx")
    doc_ends = jnp.cumsum(lengths)
    key_values = jnp.concatenate([key_rows, values], axis=1)
    pair_width = key_values.shape[1]
    local_ids = jnp.arange(block_count, dtype=jnp.int32)
    dest_dev = block_plan // block_count
    dest_slot = block_plan % block_count
    send_rank = rank_within(dest_dev, dest_slot)
    sources, occupied = slot_sources(dest_dev, send_rank, device_count, capacity)
    send_queries = pack_blocks(
        queries.reshape(block_count, BLK, query_width), sources, occupied, device_count, capacity
    )
    send_pairs = pack_blocks(
        key_values.reshape(block_count, BLK, pair_width), sources, occupied, device_count, capacity
    )
    got_queries, got_pairs = (
        lax.all_to_all(send_queries, "ctx", split_axis=0, concat_axis=0, tiled=True),
        lax.all_to_all(send_pairs, "ctx", split_axis=0, concat_axis=0, tiled=True),
    )
    root = lax.dynamic_slice_in_dim(inverse, here_index * block_count, block_count)
    from_dev = root // block_count
    recv_rank = rank_within(from_dev, local_ids)
    held_queries = unpack_blocks(got_queries, from_dev, recv_rank, capacity)
    held_pairs = unpack_blocks(got_pairs, from_dev, recv_rank, capacity)

    def key_position(key_ids):
        return jnp.take(inverse, key_ids // BLK) * BLK + key_ids % BLK

    held_att = attend_all(held_queries, held_pairs, root, doc_ends, mask_lo, key_position)
    back_sources, back_occupied = slot_sources(from_dev, recv_rank, device_count, capacity)
    send_att = pack_blocks(
        held_att.reshape(block_count, BLK, query_width),
        back_sources,
        back_occupied,
        device_count,
        capacity,
    )
    back_att = lax.all_to_all(send_att, "ctx", split_axis=0, concat_axis=0, tiled=True)
    mixed_out = project(unpack_blocks(back_att, dest_dev, send_rank, capacity), out_weight)
    return mixed_out


def solution(mesh):
    in_specs = (
        P("ctx", "head"),
        P("ctx", "head"),
        P("ctx", "head"),
        P(),
        P("ctx"),
        P(),
        P(),
        P("head", None),
    )
    out_specs = P("ctx", "head")
    return jax.shard_map(
        on_device, mesh=mesh, in_specs=in_specs, out_specs=out_specs, check_vma=False
    )
```

profile of v0, /device:TPU:1, one launch (start us, length us, event | category | flops | bytes accessed | tf_op | source)
XLA Modules:
  0.0 449.5 jit_solution(887218490249605697)
XLA Ops:
  10.5 12.6 %all-to-all-start = ((bf16[32,2,8,256]{3,2,1,0:T(8,128)(2,1)}), bf16[32,2,8,256]{3,2,1,0:T(8,128)(2,1)S(1)}, u32[]{:S(2)}, u32[]{:S(2)}) async-start(bf16[32,2,8,256]{3,2,1,0:T(8,128)(2,1)} %select_select_fusion.2), calls=%async_computation | async-start | bytes 524288 | tf_op jit(solution)/shard_map/all_to_all | solution.py:140
  24.3 11.7 %all-to-all-done = bf16[32,2,8,256]{3,2,1,0:T(8,128)(2,1)S(1)} async-done(((bf16[32,2,8,256]{3,2,1,0:T(8,128)(2,1)}), bf16[32,2,8,256]{3,2,1,0:T(8,128)(2,1)S(1)}, u32[]{:S(2)}, u32[]{:S(2)}) %all-to-all-start) | async-done | bytes 262176 | tf_op jit(solution)/shard_map/all_to_all | solution.py:140
  39.6 4.1 all-to-all-start.1
  45.2 31.0 %all-to-all-done.1 = bf16[32,2,8,1024]{3,2,1,0:T(8,128)(2,1)S(1)} async-done(((bf16[32,2,8,1024]{3,2,1,0:T(8,128)(2,1)}), bf16[32,2,8,1024]{3,2,1,0:T(8,128)(2,1)S(1)}, u32[]{:S(2)}, u32[]{:S(2)}) %all-to-all-start.1) | async-done | bytes 1048608 | tf_op jit(solution)/shard_map/all_to_all | solution.py:139
  77.1 48.6 %all-gather.2.cloned.1.call-done = bf16[8192,256]{1,0:T(8,128)(2,1)} async-done(((bf16[256,256]{1,0:T(8,128)(2,1)}), bf16[8192,256]{1,0:T(8,128)(2,1)}) %all-gather.2.cloned.1.call-update) | async-done | bytes 4194320 | tf_op jit(solution)/shard_map/all_gather | solution.py:105
  125.7 220.3 %while.21 = (s32[]{:T(128)}, f32[256,1,8]{0,2,1:T(8,128)S(1)}, f32[256,1,8]{0,2,1:T(8,128)S(1)}, f32[256,1,8,128]{0,3,2,1:T(8,128)}, s32[256]{0:T(256)S(1)}, /*i...) while((s32[]{:T(128)}, f32[256,1,8]{0,2,1:T(8,128)S(1)}, ...), condition=%wide.region_12.15_spmd.clone, body=%wide.region_8.14_spmd.clone.sunk | while | flops 276407808 | bytes 9464371 | solution.py:114
  125.8 1.4 gather_fusion
  129.1 2.5 fusion.44
  132.2 1.4 gather_fusion
  135.6 2.9 fusion.44
  142.5 2.9 fusion.44
  149.4 2.9 fusion.44
  156.3 2.9 fusion.44
  163.2 2.9 fusion.44
  170.1 2.9 fusion.44
  177.0 2.9 fusion.44
  183.9 2.9 fusion.44
  187.4 1.4 gather_fusion
  190.8 2.9 fusion.44
  197.7 2.9 fusion.44
  204.6 2.9 fusion.44
  211.5 2.9 fusion.44
  218.4 2.9 fusion.44
  225.3 2.9 fusion.44
  232.2 2.9 fusion.44
  239.0 2.9 fusion.44
  245.9 2.9 fusion.44
  249.5 1.4 gather_fusion
  252.8 2.9 fusion.44
  256.4 1.4 gather_fusion
  259.7 2.9 fusion.44
  266.6 2.9 fusion.44
  273.5 2.9 fusion.44
  280.4 2.9 fusion.44
  287.3 2.9 fusion.44
  294.2 2.9 fusion.44
  301.1 2.9 fusion.44
  308.0 2.9 fusion.44
  314.9 2.9 fusion.44
  318.5 1.4 gather_fusion
  321.8 2.9 fusion.44
  328.7 2.9 fusion.44
  335.6 2.9 fusion.44
  342.5 2.9 fusion.44
  349.7 4.6 %all-to-all-start.2 = ((bf16[32,2,8,1024]{3,2,1,0:T(8,128)(2,1)}), bf16[32,2,8,1024]{3,2,1,0:T(8,128)(2,1)S(1)}, u32[]{:S(2)}, u32[]{:S(2)}) async-start(bf16[32,2,8,1024]{3,2,1,0:T(8,128)(2,1)} %bitcast.10), calls=%async_computation.2 | async-start | bytes 2097152 | tf_op jit(solution)/shard_map/all_to_all | solution.py:160
  354.4 28.1 %all-to-all-done.2 = bf16[32,2,8,1024]{3,2,1,0:T(8,128)(2,1)S(1)} async-done(((bf16[32,2,8,1024]{3,2,1,0:T(8,128)(2,1)}), bf16[32,2,8,1024]{3,2,1,0:T(8,128)(2,1)S(1)}, u32[]{:S(2)}, u32[]{:S(2)}) %all-to-all-start.2) | async-done | bytes 1048608 | tf_op jit(solution)/shard_map/all_to_all | solution.py:160
  383.1 7.1 %convolution_convert_fusion = bf16[256,4096]{1,0:T(8,128)(2,1)} fusion(bf16[1024,4096]{1,0:T(8,128)(2,1)} %param.21, bf16[32,8,1024]{2,1,0:T(8,128)(2,1)S(1)} %gather_fusion.6, pred[32]{0:T(512)(128)(4,1)S(1)} %get-tuple-element.401), kind=kOutput, calls=%fused_computation.58 | convolution fusion | flops 2148794368 | bytes 11010080 | tf_op jit(solution)/shard_map/dot_general | solution.py:45
  390.2 52.4 %reduce-scatter.2.cloned.1.call-done = bf16[256,512]{1,0:T(8,128)(2,1)} async-done(((bf16[256,4096]{1,0:T(8,128)(2,1)}), bf16[256,512]{1,0:T(8,128)(2,1)}) %reduce-scatter.2.cloned.1.call-update) | async-done | bytes 262160 | tf_op jit(solution)/shard_map/reduce_scatter | solution.py:48
  (551 shorter events, 130.1 us)
Async XLA Ops:
  6.5 31.1 %copy-start = (bf16[256,1024]{1,0:T(8,128)(2,1)S(1)}, bf16[256,1024]{1,0:T(8,128)(2,1)}, u32[]{:S(2)}) copy-start(bf16[256,1024]{1,0:T(8,128)(2,1)} %param.14) | copy-start | bytes 1572868
  10.5 25.5 %all-to-all-start = ((bf16[32,2,8,256]{3,2,1,0:T(8,128)(2,1)}), bf16[32,2,8,256]{3,2,1,0:T(8,128)(2,1)S(1)}, u32[]{:S(2)}, u32[]{:S(2)}) async-start(bf16[32,2,8,256]{3,2,1,0:T(8,128)(2,1)} %select_select_fusion.2), calls=%async_computation | async-start | bytes 524288 | tf_op jit(solution)/shard_map/all_to_all | solution.py:140
  23.1 102.6 %all-gather.2.cloned.1.call-start = ((), (), s32[]{:S(2)}) async-start(), calls=%async_computation.4 | async-start | bytes 4325376 | tf_op jit(solution)/shard_map/all_gather | solution.py:105
  38.3 5.6 %copy-start.3 = (s32[17]{0:T(128)S(1)}, s32[17]{0:T(128)}, u32[]{:S(2)}) copy-start(s32[17]{0:T(128)} %param.17) | copy-start | bytes 208
  38.3 6.7 %copy-start.2 = (s32[1024]{0:T(1024)S(1)}, s32[1024]{0:T(1024)}, u32[]{:S(2)}) copy-start(s32[1024]{0:T(1024)} %param.20) | copy-start | bytes 12292
  39.6 36.6 %all-to-all-start.1 = ((bf16[32,2,8,1024]{3,2,1,0:T(8,128)(2,1)}), bf16[32,2,8,1024]{3,2,1,0:T(8,128)(2,1)S(1)}, u32[]{:S(2)}, u32[]{:S(2)}) async-start(bf16[32,2,8,1024]{3,2,1,0:T(8,128)(2,1)} %bitcast.7), calls=%async_computation.1 | async-start | bytes 2097152 | tf_op jit(solution)/shard_map/all_to_all | solution.py:139
  76.2 49.5 %copy-start.1 = (s32[1024]{0:T(1024)S(1)}, s32[1024]{0:T(1024)}, u32[]{:S(2)}) copy-start(s32[1024]{0:T(1024)} %param.19) | copy-start | bytes 12292
  349.7 32.8 %all-to-all-start.2 = ((bf16[32,2,8,1024]{3,2,1,0:T(8,128)(2,1)}), bf16[32,2,8,1024]{3,2,1,0:T(8,128)(2,1)S(1)}, u32[]{:S(2)}, u32[]{:S(2)}) async-start(bf16[32,2,8,1024]{3,2,1,0:T(8,128)(2,1)} %bitcast.10), calls=%async_computation.2 | async-start | bytes 2097152 | tf_op jit(solution)/shard_map/all_to_all | solution.py:160
  354.4 88.3 %reduce-scatter.2.cloned.1.call-start = ((), (), s32[]{:S(2)}) async-start(), calls=%async_computation.5 | async-start | bytes 2359296 | tf_op jit(solution)/shard_map/reduce_scatter | solution.py:48
Sparse Core Ops, SparseCore 0:
  37.6 88.1 all-gather.1
  390.3 52.2 reduce-scatter.1
where the time goes:
time: 452 us; the launch traced here: 449 us
  waiting for transfers between devices  172 us (38%)
  matrix products  143 us (32%)
  local copies, waits for them, and re-layouts  57.4 us (13%)
  other arithmetic  38.7 us (9%)
  starting transfers between devices  21.4 us (5%)
  between operations  13.7 us (3%)
    dot_general x32, matrix products, one_step(): jnp.einsum('tkgs,skd->tkgd', weights.astype(jnp.bfloat16), value_heads, p...  93.9 us
    reduce_scatter x1, waiting for transfers between devices, project(): lax.psum_scatter(partial_value, 'head', scatter_dimension=1, tiled=True)  52.4 us
    all_gather x1, waiting for transfers between devices, attend_all(): kv_piece = lax.all_gather(held_pairs, 'ctx', axis=0, tiled=True)  48.6 us
    gather x32, local copies, waits for them, and re-layouts, key_position(): return jnp.take(inverse, key_ids // BLK) * BLK + key_ids % BLK  43.7 us
    dot_general x32, matrix products, one_step(): jnp.einsum('tkgd,skd->tkgs', query_heads, key_heads, preferred_element_ty...  42.1 us
    all_to_all x1, waiting for transfers between devices, on_device(): lax.all_to_all(send_queries, 'ctx', split_axis=0, concat_axis=0, tiled=True)  31 us
    all_to_all x1, waiting for transfers between devices, on_device(): lax.all_to_all(send_att, 'ctx', split_axis=0, concat_axis=0, tiled=True)  28.1 us
    reduce_sum x32, other arithmetic, one_step(): new_sum = run_sum * fading + jnp.sum(weights, axis=-1)  16.4 us
  transfers between devices with their start and end apart: 5, of which 5 were waited for; matrix products, arithmetic and copies ran while one was open for 1% of the time, Pallas kernels for 0%

commit v1 on v0

--- a/solution.py
+++ b/solution.py
@@ -6,6 +6,12 @@
 HD = 128
 BLK = 8
 NEG_FILL = -1e30
+
+
+def _get_lanes(vector):
+    current_value = jnp.stack(tuple((vector for _ in range(jax.lax.axis_size("ctx")))))
+    f_next = jax.lax.all_to_all(current_value, "ctx", 0, 0)
+    return jnp.concatenate(f_next, 0)
 
 
 def document_of(positions, doc_ends):
@@ -102,7 +108,7 @@
         jnp.zeros(stat_shape, jnp.float32),
         jnp.zeros(stat_shape + (HD,), jnp.float32),
     )
-    kv_piece = lax.all_gather(held_pairs, "ctx", axis=0, tiled=True)
+    kv_piece = _get_lanes(held_pairs)
     piece_rows = kv_piece.shape[0]
     key_width = 256
 

time: 452 us -> 503 us (1.11)
  waiting for transfers between devices: 172 us -> 210 us
  starting transfers between devices: 21.4 us -> 30.2 us
    all_to_all x0 -> x1, waiting for transfers between devices: none -> 91.7 us  [_get_lanes(): f_next = jax.lax.all_to_all(current_value, 'ctx', 0, 0)]
    all_gather x1 -> x0, waiting for transfers between devices: 48.6 us -> none  [attend_all(): kv_piece = lax.all_gather(held_pairs, 'ctx', axis=0, tiled=True)]
    all_to_all x0 -> x1, starting transfers between devices: none -> 5.97 us  [_get_lanes(): f_next = jax.lax.all_to_all(current_value, 'ctx', 0, 0)]
where the time goes in v1:
time: 503 us; the launch traced here: 500 us
  waiting for transfers between devices  210 us (42%)
  matrix products  146 us (29%)
  local copies, waits for them, and re-layouts  59.9 us (12%)
  other arithmetic  37.3 us (7%)
  starting transfers between devices  30.2 us (6%)
  between operations  13.7 us (3%)
    dot_general x32, matrix products, one_step(): jnp.einsum('tkgs,skd->tkgd', weights.astype(jnp.bfloat16), value_heads, p...  96.7 us
    all_to_all x1, waiting for transfers between devices, _get_lanes(): f_next = jax.lax.all_to_all(current_value, 'ctx', 0, 0)  91.7 us
    reduce_scatter x1, waiting for transfers between devices, project(): lax.psum_scatter(partial_value, 'head', scatter_dimension=1, tiled=True)  52 us
    gather x32, local copies, waits for them, and re-layouts, key_position(): return jnp.take(inverse, key_ids // BLK) * BLK + key_ids % BLK  43.7 us
    dot_general x32, matrix products, one_step(): jnp.einsum('tkgd,skd->tkgs', query_heads, key_heads, preferred_element_ty...  42 us
    all_to_all x1, waiting for transfers between devices, on_device(): lax.all_to_all(send_att, 'ctx', split_axis=0, concat_axis=0, tiled=True)  28.1 us
    all_to_all x1, waiting for transfers between devices, on_device(): lax.all_to_all(send_queries, 'ctx', split_axis=0, concat_axis=0, tiled=True)  27 us
    reduce_sum x32, other arithmetic, one_step(): new_sum = run_sum * fading + jnp.sum(weights, axis=-1)  16.4 us
  transfers between devices with their start and end apart: 5, of which 5 were waited for; matrix products, arithmetic and copies ran while one was open for 1% of the time, Pallas kernels for 0%

profile of v1, /device:TPU:1, one launch (start us, length us, event | category | flops | bytes accessed | tf_op | source)
XLA Modules:
  0.0 499.7 jit_solution(6811969171896985589)
XLA Ops:
  10.5 12.6 %all-to-all-start = ((bf16[32,2,8,256]{3,2,1,0:T(8,128)(2,1)}), bf16[32,2,8,256]{3,2,1,0:T(8,128)(2,1)S(1)}, u32[]{:S(2)}, u32[]{:S(2)}) async-start(bf16[32,2,8,256]{3,2,1,0:T(8,128)(2,1)} %select_select_fusion.2), calls=%async_computation | async-start | bytes 524288 | tf_op jit(solution)/shard_map/all_to_all | solution.py:146
  25.2 10.8 %all-to-all-done = bf16[32,2,8,256]{3,2,1,0:T(8,128)(2,1)S(1)} async-done(((bf16[32,2,8,256]{3,2,1,0:T(8,128)(2,1)}), bf16[32,2,8,256]{3,2,1,0:T(8,128)(2,1)S(1)}, u32[]{:S(2)}, u32[]{:S(2)}) %all-to-all-start) | async-done | bytes 262176 | tf_op jit(solution)/shard_map/all_to_all | solution.py:146
  36.1 4.1 all-to-all-start.2
  41.4 27.0 %all-to-all-done.2 = bf16[32,2,8,1024]{3,2,1,0:T(8,128)(2,1)S(1)} async-done(((bf16[32,2,8,1024]{3,2,1,0:T(8,128)(2,1)}), bf16[32,2,8,1024]{3,2,1,0:T(8,128)(2,1)S(1)}, u32[]{:S(2)}, u32[]{:S(2)}) %all-to-all-start.2) | async-done | bytes 1048608 | tf_op jit(solution)/shard_map/all_to_all | solution.py:145
  68.4 2.4 stack.3
  70.8 6.0 %all-to-all-start.1 = ((bf16[32,256,256]{2,1,0:T(8,128)(2,1)}), bf16[32,256,256]{2,1,0:T(8,128)(2,1)}, u32[]{:S(2)}, u32[]{:S(2)}) async-start(bf16[32,256,256]{2,1,0:T(8,128)(2,1)} %stack.3), calls=%async_computation.1 | async-start | bytes 8388608 | tf_op jit(solution)/shard_map/all_to_all | solution.py:13
  79.2 91.7 %all-to-all-done.1 = bf16[32,256,256]{2,1,0:T(8,128)(2,1)} async-done(((bf16[32,256,256]{2,1,0:T(8,128)(2,1)}), bf16[32,256,256]{2,1,0:T(8,128)(2,1)}, u32[]{:S(2)}, u32[]{:S(2)}) %all-to-all-start.1) | async-done | bytes 4194336 | tf_op jit(solution)/shard_map/all_to_all | solution.py:13
  170.8 223.0 %while.21 = (s32[]{:T(128)}, f32[256,1,8]{0,2,1:T(8,128)S(1)}, f32[256,1,8]{0,2,1:T(8,128)S(1)}, f32[256,1,8,128]{0,3,2,1:T(8,128)}, s32[256]{0:T(256)S(1)}, /*i...) while((s32[]{:T(128)}, f32[256,1,8]{0,2,1:T(8,128)S(1)}, ...), condition=%wide.region_12.15_spmd.clone, body=%wide.region_8.14_spmd.clone.sunk | while | flops 276407808 | bytes 9464371 | solution.py:120
  174.2 2.6 fusion.44
  180.8 3.0 fusion.44
  184.4 1.4 gather_fusion
  187.8 3.0 fusion.44
  194.8 3.0 fusion.44
  201.7 3.0 fusion.44
  208.7 3.0 fusion.44
  215.7 3.0 fusion.44
  222.7 3.0 fusion.44
  229.7 3.0 fusion.44
  236.6 3.0 fusion.44
  240.3 1.4 gather_fusion
  243.6 3.0 fusion.44
  250.6 3.0 fusion.44
  257.6 3.0 fusion.44
  264.6 3.0 fusion.44
  271.5 3.0 fusion.44
  278.5 3.0 fusion.44
  285.5 3.0 fusion.44
  292.5 3.0 fusion.44
  296.1 1.4 gather_fusion
  299.5 3.0 fusion.44
  306.4 3.0 fusion.44
  313.4 3.0 fusion.44
  317.1 1.4 gather_fusion
  320.4 3.0 fusion.44
  327.4 3.0 fusion.44
  334.4 3.0 fusion.44
  341.4 3.0 fusion.44
  348.3 3.0 fusion.44
  355.3 3.0 fusion.44
  362.3 3.0 fusion.44
  369.3 3.0 fusion.44
  376.3 3.0 fusion.44
  383.2 3.0 fusion.44
  390.2 3.0 fusion.44
  397.5 7.5 %all-to-all-start.3 = ((bf16[32,2,8,1024]{3,2,1,0:T(8,128)(2,1)}), bf16[32,2,8,1024]{3,2,1,0:T(8,128)(2,1)S(1)}, u32[]{:S(2)}, u32[]{:S(2)}) async-start(bf16[32,2,8,1024]{3,2,1,0:T(8,128)(2,1)} %bitcast.11), calls=%async_computation.3 | async-start | bytes 2097152 | tf_op jit(solution)/shard_map/all_to_all | solution.py:166
  405.1 28.1 %all-to-all-done.3 = bf16[32,2,8,1024]{3,2,1,0:T(8,128)(2,1)S(1)} async-done(((bf16[32,2,8,1024]{3,2,1,0:T(8,128)(2,1)}), bf16[32,2,8,1024]{3,2,1,0:T(8,128)(2,1)S(1)}, u32[]{:S(2)}, u32[]{:S(2)}) %all-to-all-start.3) | async-done | bytes 1048608 | tf_op jit(solution)/shard_map/all_to_all | solution.py:166
  433.7 7.1 %convolution_convert_fusion = bf16[256,4096]{1,0:T(8,128)(2,1)} fusion(bf16[1024,4096]{1,0:T(8,128)(2,1)} %param.21, bf16[32,8,1024]{2,1,0:T(8,128)(2,1)S(1)} %gather_fusion.6, pred[32]{0:T(512)(128)(4,1)S(1)} %get-tuple-element.401), kind=kOutput, calls=%fused_computation.58 | convolution fusion | flops 2148794368 | bytes 11010080 | tf_op jit(solution)/shard_map/dot_general | solution.py:51
  440.9 52.0 %reduce-scatter.2.cloned.1.call-done = bf16[256,512]{1,0:T(8,128)(2,1)} async-done(((bf16[256,4096]{1,0:T(8,128)(2,1)}), bf16[256,512]{1,0:T(8,128)(2,1)}) %reduce-scatter.2.cloned.1.call-update) | async-done | bytes 262160 | tf_op jit(solution)/shard_map/reduce_scatter | solution.py:54
  (551 shorter events, 131.4 us)
Async XLA Ops:
  6.5 16.8 %copy-start = (bf16[256,1024]{1,0:T(8,128)(2,1)S(1)}, bf16[256,1024]{1,0:T(8,128)(2,1)}, u32[]{:S(2)}) copy-start(bf16[256,1024]{1,0:T(8,128)(2,1)} %param.14) | copy-start | bytes 1572868
  10.5 25.5 %all-to-all-start = ((bf16[32,2,8,256]{3,2,1,0:T(8,128)(2,1)}), bf16[32,2,8,256]{3,2,1,0:T(8,128)(2,1)S(1)}, u32[]{:S(2)}, u32[]{:S(2)}) async-start(bf16[32,2,8,256]{3,2,1,0:T(8,128)(2,1)} %select_select_fusion.2), calls=%async_computation | async-start | bytes 524288 | tf_op jit(solution)/shard_map/all_to_all | solution.py:146
  24.0 16.2 %copy-start.1 = (s32[1024]{0:T(1024)S(1)}, s32[1024]{0:T(1024)}, u32[]{:S(2)}) copy-start(s32[1024]{0:T(1024)} %param.19) | copy-start | bytes 12292
  36.1 32.3 %all-to-all-start.2 = ((bf16[32,2,8,1024]{3,2,1,0:T(8,128)(2,1)}), bf16[32,2,8,1024]{3,2,1,0:T(8,128)(2,1)S(1)}, u32[]{:S(2)}, u32[]{:S(2)}) async-start(bf16[32,2,8,1024]{3,2,1,0:T(8,128)(2,1)} %bitcast.8), calls=%async_computation.2 | async-start | bytes 2097152 | tf_op jit(solution)/shard_map/all_to_all | solution.py:145
  70.8 6.2 %copy-start.3 = (s32[17]{0:T(128)S(1)}, s32[17]{0:T(128)}, u32[]{:S(2)}) copy-start(s32[17]{0:T(128)} %param.17) | copy-start | bytes 208
  70.8 7.3 %copy-start.2 = (s32[1024]{0:T(1024)S(1)}, s32[1024]{0:T(1024)}, u32[]{:S(2)}) copy-start(s32[1024]{0:T(1024)} %param.20) | copy-start | bytes 12292
  70.8 100.0 %all-to-all-start.1 = ((bf16[32,256,256]{2,1,0:T(8,128)(2,1)}), bf16[32,256,256]{2,1,0:T(8,128)(2,1)}, u32[]{:S(2)}, u32[]{:S(2)}) async-start(bf16[32,256,256]{2,1,0:T(8,128)(2,1)} %stack.3), calls=%async_computation.1 | async-start | bytes 8388608 | tf_op jit(solution)/shard_map/all_to_all | solution.py:13
  397.5 35.6 %all-to-all-start.3 = ((bf16[32,2,8,1024]{3,2,1,0:T(8,128)(2,1)}), bf16[32,2,8,1024]{3,2,1,0:T(8,128)(2,1)S(1)}, u32[]{:S(2)}, u32[]{:S(2)}) async-start(bf16[32,2,8,1024]{3,2,1,0:T(8,128)(2,1)} %bitcast.11), calls=%async_computation.3 | async-start | bytes 2097152 | tf_op jit(solution)/shard_map/all_to_all | solution.py:166
  405.0 87.9 %reduce-scatter.2.cloned.1.call-start = ((), (), s32[]{:S(2)}) async-start(), calls=%async_computation.5 | async-start | bytes 2359296 | tf_op jit(solution)/shard_map/reduce_scatter | solution.py:54
Sparse Core Ops, SparseCore 0:
  441.0 51.8 reduce-scatter.1
